TPU v7x, 32 devices: a whole 2x2x4 slice. The times are simulated.
32 devices in a mesh: groups: 2 (over x), ctx: 8 (over z, y), exp: 2 (over core).
Axes of the slice: x: 2, y: 2, z: 4, core: 2. Of those that a mesh axis runs over, the one named last changes fastest.
Arguments:
- tokens: bfloat16 [2048, 5120], P(('groups', 'ctx'), 'exp'), parts along dimension 0, may hold values from -6 to 6
- route_ids: int32 [2048, 2], P(('groups', 'ctx')), parts along dimension 0, may hold values from 0 to 3, all different within a row; in each aligned block of 128 rows (0 to 127, 128 to 255, ...) at most 128 rows name the same one
- route_gates: float32 [2048, 2], P(('groups', 'ctx')), parts along dimension 0, may hold values from 0.2 to 1
- w_in: bfloat16 [8, 5120, 1536], P('ctx', 'exp'), may hold values from -0.078125 to 0.078125
- w_out: bfloat16 [8, 768, 5120], P('ctx', None, 'exp'), may hold values from -0.15625 to 0.15625
Outputs:
- mixed: bfloat16 [2048, 5120], P(('groups', 'ctx'), 'exp'), parts along dimension 0
There are 2 independent parts, one for each index of `groups`. A program takes and returns all parts, laid end to end along the dimension named above; an argument that names none is the same for every part. Nothing has to cross between parts.
Inputs may be any that keep to these rules, and one draw needn't show every extreme that they name: `route_ids`: within the 128 rows of one device no expert is named more than 128 times, a bound that some block reaches; the ids of one token differ.
All inputs are finite; a program needn't handle non-finite values.
Results may differ from a plain program's by a relative error of at most 0.025.
Values may be sent and summed in bfloat16 or wider, within the bound.
A program may use at most 64 MiB of HBM per device.

v0:
```python
import jax
import jax.numpy as jnp
from jax import lax
from jax.sharding import PartitionSpec as P


def expert_half(rows, w_in, w_out):
    gate_up = jnp.dot(rows, w_in[0], preferred_element_type=jnp.float32)
    summed = lax.psum(gate_up.astype(jnp.bfloat16), "exp").astype(jnp.float32)
    hidden_units = w_out.shape[1]
    hidden = (jax.nn.silu(summed[:, :hidden_units]) * summed[:, hidden_units:]).astype(jnp.bfloat16)
    return jnp.dot(hidden, w_out[0], preferred_element_type=jnp.float32).astype(jnp.bfloat16)


def gate_table(route_ids, route_gates, experts):
    named = route_ids[:, :, None] == jnp.arange(experts, dtype=jnp.int32)
    return jnp.sum(jnp.where(named, route_gates[:, :, None], 0.0), axis=1)


def dense(tokens, route_ids, route_gates, w_in, w_out):
    experts = lax.axis_size("ctx") // 2
    gates = lax.all_gather(gate_table(route_ids, route_gates, experts), "ctx", axis=0, tiled=True)
    gate = lax.dynamic_slice_in_dim(gates, lax.axis_index("ctx") // 2, 1, axis=1)
    rows = lax.all_gather(tokens, "ctx", axis=0, tiled=True)
    out = (expert_half(rows, w_in, w_out).astype(jnp.float32) * gate).astype(jnp.bfloat16)
    return lax.psum_scatter(out, "ctx", scatter_dimension=0, tiled=True)


def per_device(tokens, route_ids, route_gates, w_in, w_out):
    ctx_size = lax.axis_size("ctx")
    experts = ctx_size // 2
    tok_rows, half_width = tokens.shape
    top_count = route_ids.shape[1]
    capacity = 2 * ((top_count * tok_rows + experts - 1) // experts)
    if capacity >= tok_rows:
        return dense(tokens, route_ids, route_gates, w_in, w_out)
    slots = experts * capacity
    flat_ids = route_ids.reshape(-1)
    onehot = (flat_ids[:, None] == jnp.arange(experts, dtype=jnp.int32)[None, :]).astype(jnp.int32)
    before = jnp.cumsum(onehot, axis=0) - onehot
    rank = jnp.sum(before * onehot, axis=1)
    slot_of = flat_ids * capacity + rank
    placed = (slot_of[:, None] == jnp.arange(slots, dtype=jnp.int32)[None, :]).astype(jnp.bfloat16)
    placed = placed.reshape(tok_rows, top_count, slots)
    every_map = jnp.sum(placed.astype(jnp.float32), axis=1).astype(jnp.bfloat16)
    gathered = lax.dot_general(
        every_map, tokens, (((0,), (0,)), ((), ())), preferred_element_type=jnp.float32
    ).astype(jnp.bfloat16)
    outgoing = jnp.broadcast_to(
        gathered.reshape(experts, 1, capacity, half_width), (experts, 2, capacity, half_width)
    ).reshape(ctx_size, capacity, half_width)
    received = lax.all_to_all(outgoing, "ctx", split_axis=0, concat_axis=0, tiled=True)
    count = received.shape[1]
    partial_out = expert_half(received.reshape(-1, half_width), w_in, w_out).reshape(
        ctx_size, count, half_width
    )
    returned = lax.all_to_all(partial_out, "ctx", split_axis=0, concat_axis=0, tiled=True)
    results = (
        jnp.sum(returned.astype(jnp.float32).reshape(experts, 2, capacity, half_width), axis=1)
        .astype(jnp.bfloat16)
        .reshape(slots, half_width)
    )
    mixed = jnp.zeros((tok_rows, half_width), jnp.float32)
    for route in range(top_count):
        route_out = jnp.dot(placed[:, route], results, preferred_element_type=jnp.float32)
        mixed = mixed + route_gates[:, route : route + 1] * route_out
    return mixed.astype(jnp.bfloat16)


def solution(mesh):
    placed = (
        P(("groups", "ctx"), "exp"),
        P(("groups", "ctx"), None),
        P(("groups", "ctx"), None),
        P("ctx", "exp", None),
        P("ctx", None, "exp"),
    )
    return jax.shard_map(
        per_device,
        mesh=mesh,
        in_specs=placed,
        out_specs=P(("groups", "ctx"), "exp"),
        check_vma=False,
    )
```

profile of v0, /device:TPU:0, one launch (start us, length us, event | category | flops | bytes accessed | tf_op | source)
XLA Modules:
  0.0 253.9 jit_solution(14668510302520521451)
XLA Ops:
  6.5 0.0 all-gather.2.cloned.1.call-start
  6.5 0.7 all-gather.2.cloned.1.call-update
  7.3 0.0 copy-start
  7.3 0.0 copy-start.1
  7.3 0.0 all-reduce.2.cloned.1.call-start
  7.3 90.8 %all-gather.2.cloned.1.call-done = bf16[1024,2560]{1,0:T(8,128)(2,1)} async-done(((bf16[128,2560]{1,0:T(8,128)(2,1)}), bf16[1024,2560]{1,0:T(8,128)(2,1)}) %all-gather.2.cloned.1.call-update) | async-done | bytes 5242896 | tf_op jit(solution)/shard_map/all_gather | solution.py:24
  98.2 13.3 %fusion.3 = bf16[1024,1536]{1,0:T(8,128)(2,1)} fusion(bf16[1024,2560]{1,0:T(8,128)(2,1)} %all-gather.2.cloned.1.call-done, bf16[1,2560,1536]{2,1,0:T(8,128)(2,1)} %param.8), kind=kOutput, calls=%fused_computation.5 | convolution fusion | flops 8054636544 | bytes 16252928 | tf_op jit(solution)/shard_map/dot_general | solution.py:8
  111.5 0.0 all-reduce.2.cloned.1.call-update
  111.5 0.0 reduce-scatter.2.cloned.1.call-start
  111.6 0.0 copy-done
  111.6 0.0 copy-done.1
  111.6 26.1 %all_gather.7 = f32[1024,4]{0,1:T(4,128)S(1)} all-gather(f32[128,4]{0,1:T(4,128)S(1)} %select_reduce_fusion), channel_id=1, replica_groups=mesh['groups'=2,'ctx'=8,'exp'=2] {'ctx'}, dimensions={0}, use_global_device_ids=true | all-gather | bytes 18432 | tf_op jit(solution)/shard_map/all_gather | solution.py:22
  137.7 0.0 all-reduce.2.cloned.1.call-done
  137.8 0.0 copy-start.2
  137.8 2.9 %convert_element_type.19 = f32[1024,1536]{1,0:T(8,128)S(1)} convert(bf16[1024,1536]{1,0:T(8,128)(2,1)} %all-reduce.2.cloned.1.call-done) | non-fusion elementwise | flops 1572864 | bytes 9437184 | tf_op jit(solution)/shard_map/convert_element_type | solution.py:9
  140.7 0.1 copy-done.2
  140.8 6.1 %multiply_convert_fusion = bf16[1024,2560]{1,0:T(8,128)(2,1)} fusion(f32[1024]{0:T(1024)S(1)} %bitcast.10, bf16[1,768,2560]{2,1,0:T(8,128)(2,1)S(1)} %copy-done.2, f32[1024,1536]{1,0:T(8,128)S(1)} %convert_element_type.19), kind=kOutput, calls=%fused_computation | convolution fusion | flops 4041736192 | bytes 15470592 | tf_op jit(solution)/shard_map/dot_general | solution.py:12
  146.9 0.0 reduce-scatter.2.cloned.1.call-update
  146.9 100.4 %reduce-scatter.2.cloned.1.call-done = bf16[128,2560]{1,0:T(8,128)(2,1)} async-done(((bf16[1024,2560]{1,0:T(8,128)(2,1)}), bf16[128,2560]{1,0:T(8,128)(2,1)}) %reduce-scatter.2.cloned.1.call-update) | async-done | bytes 655376 | tf_op jit(solution)/shard_map/reduce_scatter | solution.py:26
  (2 shorter events, 0.0 us)
Async XLA Ops:
  6.5 91.6 %all-gather.2.cloned.1.call-start = ((), (), s32[]{:S(2)}) async-start(), calls=%async_computation.1 | async-start | bytes 5898240 | tf_op jit(solution)/shard_map/all_gather | solution.py:24
  7.3 104.3 %copy-start = (f32[128,2]{0,1:T(2,128)S(1)}, f32[128,2]{0,1:T(2,128)}, u32[]{:S(2)}) copy-start(f32[128,2]{0,1:T(2,128)} %param.7) | copy-start | bytes 3076
  7.3 104.3 %copy-start.1 = (s32[128,2]{0,1:T(2,128)S(1)}, s32[128,2]{0,1:T(2,128)}, u32[]{:S(2)}) copy-start(s32[128,2]{0,1:T(2,128)} %param.6) | copy-start | bytes 3076
  7.3 130.5 %all-reduce.2.cloned.1.call-start = ((), (), s32[]{:S(2)}) async-start(), calls=%async_computation.2 | async-start | bytes 6291456 | tf_op jit(solution)/shard_map/psum | solution.py:9
  111.5 135.9 %reduce-scatter.2.cloned.1.call-start = ((), (), s32[]{:S(2)}) async-start(), calls=%async_computation.3 | async-start | bytes 5898240 | tf_op jit(solution)/shard_map/reduce_scatter | solution.py:26
  137.8 3.1 %copy-start.2 = (bf16[1,768,2560]{2,1,0:T(8,128)(2,1)S(1)}, bf16[1,768,2560]{2,1,0:T(8,128)(2,1)}, u32[]{:S(2)}) copy-start(bf16[1,768,2560]{2,1,0:T(8,128)(2,1)} %param.9) | copy-start | bytes 11796484
Sparse Core Ops, SparseCore 0:
  9.5 88.5 all-gather.1
  111.6 21.4 all-reduce.1
  147.1 100.2 reduce-scatter.1
where the time goes:
time: 254 us
  waiting for transfers between devices  192 us (76%)
  blocking collectives  26.1 us (10%)
  matrix products  19.4 us (8%)
  between operations  13.2 us (5%)
  other arithmetic  2.91 us (1%)
    reduce_scatter x1, waiting for transfers between devices, dense(): return lax.psum_scatter(out, 'ctx', scatter_dimension=0, tiled=True)  100 us
    all_gather x1, waiting for transfers between devices, dense(): rows = lax.all_gather(tokens, 'ctx', axis=0, tiled=True)  90.8 us
    all_gather x1, blocking collectives, dense(): lax.all_gather(gate_table(route_ids, route_gates, experts), 'ctx', axis=0...  26.1 us
    dot_general x1, matrix products, expert_half(): gate_up = jnp.dot(rows, w_in[0], preferred_element_type=jnp.float32)  13.3 us
    dot_general x1, matrix products, expert_half(): jnp.dot(hidden, w_out[0], preferred_element_type=jnp.float32)  6.08 us
  transfers between devices with their start and end apart: 3, of which 2 were waited for; matrix products, arithmetic and copies ran while one was open for 0% of the time, Pallas kernels for 0%

commit v1 on v0

--- a/solution.py
+++ b/solution.py
@@ -19,7 +19,9 @@
 
 def dense(tokens, route_ids, route_gates, w_in, w_out):
     experts = lax.axis_size("ctx") // 2
-    gates = lax.all_gather(gate_table(route_ids, route_gates, experts), "ctx", axis=0, tiled=True)
+    part = gate_table(route_ids, route_gates, experts)
+    sent = jnp.stack([part] * lax.axis_size("ctx"))
+    gates = jnp.concatenate(lax.all_to_all(sent, "ctx", 0, 0), axis=0)
     gate = lax.dynamic_slice_in_dim(gates, lax.axis_index("ctx") // 2, 1, axis=1)
     rows = lax.all_gather(tokens, "ctx", axis=0, tiled=True)
     out = (expert_half(rows, w_in, w_out).astype(jnp.float32) * gate).astype(jnp.bfloat16)

time: 254 us -> 253 us (level)
  blocking collectives: 26.1 us -> 0 us
  waiting for transfers between devices: 192 us -> 213 us
  starting transfers between devices: 0.08 us -> 3.42 us
    all_gather x1 -> x0, blocking collectives: 26.1 us -> none  [dense(): lax.all_gather(gate_table(route_ids, route_gates, experts), 'ctx', axis=0...]
    psum x1, waiting for transfers between devices: 0.02 us -> 11.1 us  [expert_half(): summed = lax.psum(gate_up.astype(jnp.bfloat16), 'exp').astype(jnp.float32)]
    all_to_all x0 -> x1, waiting for transfers between devices: none -> 6.45 us  [dense(): gates = jnp.concatenate(lax.all_to_all(sent, 'ctx', 0, 0), axis=0)]
    reduce_scatter x1, waiting for transfers between devices: 100 us -> 104 us  [dense(): return lax.psum_scatter(out, 'ctx', scatter_dimension=0, tiled=True)]
    all_to_all x0 -> x1, starting transfers between devices: none -> 3.34 us  [dense(): gates = jnp.concatenate(lax.all_to_all(sent, 'ctx', 0, 0), axis=0)]
  transfers between devices with their start and end apart: 3 -> 4, of which waited for: 2 -> 4; matrix products, arithmetic and copies ran while one was open for 0% -> 0% of each run, Pallas kernels for 0% -> 0%
where the time goes in v1:
time: 253 us
  waiting for transfers between devices  213 us (84%)
  matrix products  19.5 us (8%)
  between operations  13.2 us (5%)
  starting transfers between devices  3.42 us (1%)
  other arithmetic  2.91 us (1%)
    reduce_scatter x1, waiting for transfers between devices, dense(): return lax.psum_scatter(out, 'ctx', scatter_dimension=0, tiled=True)  104 us
    all_gather x1, waiting for transfers between devices, dense(): rows = lax.all_gather(tokens, 'ctx', axis=0, tiled=True)  90.8 us
    dot_general x1, matrix products, expert_half(): gate_up = jnp.dot(rows, w_in[0], preferred_element_type=jnp.float32)  13.4 us
    psum x1, waiting for transfers between devices, expert_half(): summed = lax.psum(gate_up.astype(jnp.bfloat16), 'exp').astype(jnp.float32)  11.1 us
    all_to_all x1, waiting for transfers between devices, dense(): gates = jnp.concatenate(lax.all_to_all(sent, 'ctx', 0, 0), axis=0)  6.45 us
    dot_general x1, matrix products, expert_half(): jnp.dot(hidden, w_out[0], preferred_element_type=jnp.float32)  6.12 us
  transfers between devices with their start and end apart: 4, of which 4 were waited for; matrix products, arithmetic and copies ran while one was open for 0% of the time, Pallas kernels for 0%

profile of v1, /device:TPU:0, one launch (start us, length us, event | category | flops | bytes accessed | tf_op | source)
XLA Modules:
  0.0 253.3 jit_solution(2102381414069161173)
XLA Ops:
  6.5 0.0 all-gather.2.cloned.1.call-start
  6.5 0.7 all-gather.2.cloned.1.call-update
  7.3 0.0 copy-start
  7.3 0.0 copy-start.1
  7.3 0.0 all-reduce.2.cloned.1.call-start
  7.3 90.8 %all-gather.2.cloned.1.call-done = bf16[1024,2560]{1,0:T(8,128)(2,1)} async-done(((bf16[128,2560]{1,0:T(8,128)(2,1)}), bf16[1024,2560]{1,0:T(8,128)(2,1)}) %all-gather.2.cloned.1.call-update) | async-done | bytes 5242896 | tf_op jit(solution)/shard_map/all_gather | solution.py:26
  98.2 13.4 %fusion.3 = bf16[1024,1536]{1,0:T(8,128)(2,1)} fusion(bf16[1024,2560]{1,0:T(8,128)(2,1)} %all-gather.2.cloned.1.call-done, bf16[1,2560,1536]{2,1,0:T(8,128)(2,1)} %param.8), kind=kOutput, calls=%fused_computation.5 | convolution fusion | flops 8054636544 | bytes 16252928 | tf_op jit(solution)/shard_map/dot_general | solution.py:8
  111.6 0.0 all-reduce.2.cloned.1.call-update
  111.6 0.0 copy-done
  111.6 0.0 copy-done.1
  111.6 0.6 stack.2
  112.2 3.3 %all-to-all-start = ((f32[8,128,4]{1,2,0:T(4,128)}), f32[8,128,4]{1,2,0:T(4,128)S(1)}, u32[]{:S(2)}, u32[]{:S(2)}) async-start(f32[8,128,4]{1,2,0:T(4,128)} %stack.2), calls=%async_computation | async-start | bytes 32768 | tf_op jit(solution)/shard_map/all_to_all | solution.py:24
  115.6 0.0 reduce-scatter.2.cloned.1.call-start
  115.7 6.4 %all-to-all-done = f32[8,128,4]{1,2,0:T(4,128)S(1)} async-done(((f32[8,128,4]{1,2,0:T(4,128)}), f32[8,128,4]{1,2,0:T(4,128)S(1)}, u32[]{:S(2)}, u32[]{:S(2)}) %all-to-all-start) | async-done | bytes 16416 | tf_op jit(solution)/shard_map/all_to_all | solution.py:24
  122.1 11.1 %all-reduce.2.cloned.1.call-done = bf16[1024,1536]{1,0:T(8,128)(2,1)} async-done(((bf16[1024,1536]{1,0:T(8,128)(2,1)}), bf16[1024,1536]{1,0:T(8,128)(2,1)}) %all-reduce.2.cloned.1.call-update) | async-done | bytes 3145744 | tf_op jit(solution)/shard_map/psum | solution.py:9
  133.3 0.0 copy-start.2
  133.3 2.9 %convert_element_type.19 = f32[1024,1536]{1,0:T(8,128)S(1)} convert(bf16[1024,1536]{1,0:T(8,128)(2,1)} %all-reduce.2.cloned.1.call-done) | non-fusion elementwise | flops 1572864 | bytes 9437184 | tf_op jit(solution)/shard_map/convert_element_type | solution.py:9
  136.2 0.1 copy-done.2
  136.3 6.1 %multiply_convert_fusion = bf16[1024,2560]{1,0:T(8,128)(2,1)} fusion(f32[1024]{0:T(1024)S(1)} %bitcast.12, bf16[1,768,2560]{2,1,0:T(8,128)(2,1)S(1)} %copy-done.2, f32[1024,1536]{1,0:T(8,128)S(1)} %convert_element_type.19), kind=kOutput, calls=%fused_computation | convolution fusion | flops 4041736192 | bytes 15470592 | tf_op jit(solution)/shard_map/dot_general | solution.py:12
  142.4 0.0 reduce-scatter.2.cloned.1.call-update
  142.5 104.3 %reduce-scatter.2.cloned.1.call-done = bf16[128,2560]{1,0:T(8,128)(2,1)} async-done(((bf16[1024,2560]{1,0:T(8,128)(2,1)}), bf16[128,2560]{1,0:T(8,128)(2,1)}) %reduce-scatter.2.cloned.1.call-update) | async-done | bytes 655376 | tf_op jit(solution)/shard_map/reduce_scatter | solution.py:28
  (2 shorter events, 0.0 us)
Async XLA Ops:
  6.5 91.6 %all-gather.2.cloned.1.call-start = ((), (), s32[]{:S(2)}) async-start(), calls=%async_computation.2 | async-start | bytes 5898240 | tf_op jit(solution)/shard_map/all_gather | solution.py:26
  7.3 104.3 %copy-start = (f32[128,2]{0,1:T(2,128)S(1)}, f32[128,2]{0,1:T(2,128)}, u32[]{:S(2)}) copy-start(f32[128,2]{0,1:T(2,128)} %param.7) | copy-start | bytes 3076
  7.3 104.3 %copy-start.1 = (s32[128,2]{0,1:T(2,128)S(1)}, s32[128,2]{0,1:T(2,128)}, u32[]{:S(2)}) copy-start(s32[128,2]{0,1:T(2,128)} %param.6) | copy-start | bytes 3076
  7.3 126.0 %all-reduce.2.cloned.1.call-start = ((), (), s32[]{:S(2)}) async-start(), calls=%async_computation.3 | async-start | bytes 6291456 | tf_op jit(solution)/shard_map/psum | solution.py:9
  112.2 9.9 %all-to-all-start = ((f32[8,128,4]{1,2,0:T(4,128)}), f32[8,128,4]{1,2,0:T(4,128)S(1)}, u32[]{:S(2)}, u32[]{:S(2)}) async-start(f32[8,128,4]{1,2,0:T(4,128)} %stack.2), calls=%async_computation | async-start | bytes 32768 | tf_op jit(solution)/shard_map/all_to_all | solution.py:24
  115.6 131.2 %reduce-scatter.2.cloned.1.call-start = ((), (), s32[]{:S(2)}) async-start(), calls=%async_computation.4 | async-start | bytes 5898240 | tf_op jit(solution)/shard_map/reduce_scatter | solution.py:28
  133.3 3.1 %copy-start.2 = (bf16[1,768,2560]{2,1,0:T(8,128)(2,1)S(1)}, bf16[1,768,2560]{2,1,0:T(8,128)(2,1)}, u32[]{:S(2)}) copy-start(bf16[1,768,2560]{2,1,0:T(8,128)(2,1)} %param.9) | copy-start | bytes 11796484
Sparse Core Ops, SparseCore 0:
  9.5 88.5 all-gather.1
  111.7 21.4 all-reduce.1
  142.6 104.1 reduce-scatter.1
